TPU v7x, 512 devices: a whole 4x8x8 slice. The times are simulated.
512 devices in a mesh: dp: 32 (over y, z_hi), seq: 16 (over x, z_lo, core).
Axes of the slice: x: 4, y: 8, z: 8 (z_hi: 4, z_lo: 2; z = z_hi * 2 + z_lo), core: 2. Of those that a mesh axis runs over, the one named last changes fastest.
Arguments:
- queries: bfloat16 [32, 2048, 2048], P('dp', 'seq'), may hold values from -6 to 6
- grad_out: bfloat16 [32, 2048, 2048], P('dp', 'seq'), may hold values from -6 to 6
- encoded: bfloat16 [32, 32, 64, 896], P('dp', 'seq'), may hold values from -6 to 6
- kv_weight: bfloat16 [896, 4096], P(None, 'dp'), may hold values from -0.1875 to 0.1875
- neighbour_ids: int32 [32, 32, 2], P('dp', 'seq'), may hold values from 0 to 31, all different within a row
- slot_map: int32 [32, 32], P('dp'), may hold values from 0 to 31, each once within a row
Outputs:
- attended: bfloat16 [32, 2048, 2048], P('dp', 'seq')
- grad_queries: bfloat16 [32, 2048, 2048], P('dp', 'seq')
- grad_encoded: float32 [32, 32, 64, 896], P('dp', 'seq')
Inputs may be any that keep to these rules, and one draw needn't show every extreme that they name: `neighbour_ids`: each span names 2 different neighbour ids of its own sequence. `slot_map`: for each sequence a permutation; storage position p lies on the seq index p // 2.
All inputs are finite; a program needn't handle non-finite values.
Results may differ from a plain program's by a relative error of at most 0.018.
Values may be sent and summed in bfloat16 or wider, within the bound.
A program may use at most 64 MiB of HBM per device.

v0:
```python
import jax
import jax.numpy as jnp
from jax import lax
from jax.sharding import PartitionSpec as P

HEAD_SIZE = 128
HEADS = 16
SPAN = 64
NLEN = 64
READS = 2


def lookup_positions(neighbour_ids, slot_map):
    pool_size = slot_map.shape[1]
    matches = neighbour_ids[0][:, :, None] == jnp.arange(pool_size, dtype=jnp.int32)[None, None, :]
    positions = jnp.sum(jnp.where(matches, slot_map[0][None, None, :], 0), axis=2)
    return positions.reshape(-1)


def per_device(queries, grad_out, encoded, kv_weight, neighbour_ids, slot_map):
    hidden = HEADS * HEAD_SIZE
    scale_factor = HEAD_SIZE ** (-0.5)
    spans = queries.shape[1] // SPAN
    pool_size = slot_map.shape[1]
    width_enc = encoded.shape[3]
    flat_pos = lookup_positions(neighbour_ids, slot_map)
    read_count = flat_pos.shape[0]
    read_rows = read_count * NLEN
    pool_rows = lax.all_gather(encoded, "seq", axis=1, tiled=True)[0]
    picked = jnp.take(pool_rows, flat_pos, axis=0).reshape(read_rows, width_enc)
    whole_weight = lax.all_gather(kv_weight, "dp", axis=1, tiled=True)
    kv_flat = jnp.dot(picked, whole_weight, preferred_element_type=jnp.float32).astype(jnp.bfloat16)
    kv_spans = kv_flat.reshape(spans, READS * NLEN, 2 * hidden)
    keys = kv_spans[:, :, :hidden].reshape(spans, READS * NLEN, HEADS, HEAD_SIZE)
    values = kv_spans[:, :, hidden:].reshape(spans, READS * NLEN, HEADS, HEAD_SIZE)
    query_tiles = queries[0].reshape(spans, SPAN, HEADS, HEAD_SIZE)
    grad_tiles = grad_out[0].reshape(spans, SPAN, HEADS, HEAD_SIZE)
    scores = (
        jnp.einsum("cqhd,ckhd->chqk", query_tiles, keys, preferred_element_type=jnp.float32)
        * scale_factor
    )
    expos = jnp.exp(scores)
    probs = expos / jnp.sum(expos, axis=-1, keepdims=True)
    probs_low = probs.astype(jnp.bfloat16)
    attended = jnp.einsum("chqk,ckhd->cqhd", probs_low, values, preferred_element_type=jnp.float32)
    attended = attended.astype(jnp.bfloat16).reshape(1, spans * SPAN, hidden)
    d_probs = jnp.einsum("cqhd,ckhd->chqk", grad_tiles, values, preferred_element_type=jnp.float32)
    delta = jnp.sum(probs * d_probs, axis=-1, keepdims=True)
    d_scores = (probs * (d_probs - delta) * scale_factor).astype(jnp.bfloat16)
    grad_queries = jnp.einsum("chqk,ckhd->cqhd", d_scores, keys, preferred_element_type=jnp.float32)
    grad_queries = grad_queries.astype(jnp.bfloat16).reshape(1, spans * SPAN, hidden)
    d_keys = jnp.einsum(
        "chqk,cqhd->ckhd", d_scores, query_tiles, preferred_element_type=jnp.float32
    )
    d_values = jnp.einsum(
        "chqk,cqhd->ckhd", probs_low, grad_tiles, preferred_element_type=jnp.float32
    )
    grad_reads = jnp.concatenate(
        [d_keys.reshape(read_rows, hidden), d_values.reshape(read_rows, hidden)], axis=-1
    ).astype(jnp.bfloat16)
    enc_reads = lax.dot_general(
        grad_reads, whole_weight, (((1,), (1,)), ((), ())), preferred_element_type=jnp.float32
    )
    enc_reads = enc_reads.reshape(read_count, NLEN, width_enc)
    onehot = (flat_pos[:, None] == jnp.arange(pool_size, dtype=jnp.int32)[None, :]).astype(
        jnp.float32
    )
    partial_value = jnp.einsum("rn,rlk->nlk", onehot, enc_reads, precision=lax.Precision.HIGHEST)
    rounded = lax.optimization_barrier(partial_value.astype(jnp.bfloat16))
    grad_encoded = lax.psum_scatter(
        rounded.astype(jnp.float32)[None].astype(jnp.bfloat16),
        "seq",
        scatter_dimension=1,
        tiled=True,
    ).astype(jnp.float32)
    return (attended, grad_queries, grad_encoded)


def solution(mesh):
    in_specs = (
        P("dp", "seq", None),
        P("dp", "seq", None),
        P("dp", "seq", None, None),
        P(None, "dp"),
        P("dp", "seq", None),
        P("dp", None),
    )
    out_specs = (P("dp", "seq", None), P("dp", "seq", None), P("dp", "seq", None, None))
    return jax.shard_map(
        per_device, mesh=mesh, in_specs=in_specs, out_specs=out_specs, check_vma=False
    )
```

profile of v0, /device:TPU:16, one launch (start us, length us, event | category | flops | bytes accessed | tf_op | source)
XLA Modules:
  0.0 315.2 jit_solution(13738438806581832548)
XLA Ops:
  7.2 0.0 all-gather.3.cloned.1.call-start
  7.2 0.7 all-gather.3.cloned.1.call-update
  7.9 0.0 all-gather.5.cloned.1.call-start
  7.9 0.7 all-gather.5.cloned.1.call-update
  8.6 0.0 reduce-scatter.2.cloned.1.call-start
  8.7 0.9 fusion.30
  9.6 0.1 reshape.81
  9.7 0.1 reshape.80
  9.8 0.1 broadcast_in_dim.36
  9.9 0.1 broadcast_in_dim.37
  9.9 1.2 copy.73
  11.1 1.1 copy.74
  12.3 44.6 %all-gather.3.cloned.1.call-done = bf16[1,32,64,896]{3,2,0,1:T(8,128)(2,1)} async-done(((bf16[1,2,64,896]{3,2,0,1:T(8,128)(2,1)}), bf16[1,32,64,896]{3,2,0,1:T(8,128)(2,1)}) %all-gather.3.cloned.1.call-update) | async-done | bytes 3670032 | tf_op jit(solution)/shard_map/all_gather | solution.py:29
  56.8 2.7 gather_fusion
  59.5 0.1 bitcast_select_fusion
  59.6 140.9 %all-gather.5.cloned.1.call-done = bf16[896,4096]{1,0:T(8,128)(2,1)} async-done(((bf16[896,128]{1,0:T(8,128)(2,1)}), bf16[896,4096]{1,0:T(8,128)(2,1)}) %all-gather.5.cloned.1.call-update) | async-done | bytes 7340048 | tf_op jit(solution)/shard_map/all_gather | solution.py:31
  200.5 5.4 %convolution_convert_fusion = bf16[256,4096]{1,0:T(8,128)(2,1)S(1)} fusion(bf16[256,896]{1,0:T(8,128)(2,1)S(1)} %bitcast_select_fusion, bf16[896,4096]{1,0:T(8,128)(2,1)} %all-gather.5.cloned.1.call-done), kind=kOutput, calls=%fused_computation.2 | convolution fusion | flops 1880096768 | bytes 9895936 | tf_op jit(solution)/shard_map/dot_general | solution.py:32
  206.0 1.3 fusion.42
  207.2 0.7 copy.71
  207.9 0.0 copy-start
  207.9 2.0 copy.72
  209.9 0.4 fusion.11
  210.3 0.0 copy-start.2
  210.3 1.1 copy-done.2
  211.4 1.3 fusion.23
  212.7 3.5 %fusion.6 = bf16[2,128,16,128]{3,1,2,0:T(8,128)(2,1)} fusion(bf16[2,64,16,128]{3,2,1,0:T(8,128)(2,1)S(1)} %bitcast.70, f32[2,16,64,128]{3,2,1,0:T(8,128)} %copy-done.2), kind=kOutput, calls=%fused_computation.11 | convolution fusion | flops 68159616 | bytes 2621440 | tf_op jit(solution)/shard_map/chqk,cqhd->ckhd/dot_general | solution.py:55
  216.2 0.0 copy-done
  216.2 1.4 convolution_bitcast_fusion
  217.6 3.0 copy.63
  220.6 2.9 fusion.5
  223.5 0.7 copy.61
  224.2 1.7 copy_bitcast_fusion
  225.9 5.7 %fusion.1 = f32[256,896]{1,0:T(8,128)S(1)} fusion(bf16[896,4096]{1,0:T(8,128)(2,1)} %all-gather.5.cloned.1.call-done, bf16[256,2048]{1,0:T(8,128)(2,1)S(1)} %get-tuple-element.17, bf16[256,2048]{1,0:T(8,128)(2,1)S(1)} %get-tuple-element.18), kind=kOutput, calls=%fused_computation.4 | convolution fusion | flops 1883242496 | bytes 10354688 | tf_op jit(solution)/shard_map/dot_general | solution.py:61
  231.6 3.8 %convolution_convert_fusion.1 = bf16[32,64,896]{2,0,1:T(8,128)(2,1)S(1)} fusion(f32[4,64,896]{2,1,0:T(8,128)S(1)} %bitcast.73, s32[4]{0:T(128)S(1)} %reshape.80), kind=kOutput, calls=%fused_computation.3 | convolution fusion | flops 89915520 | bytes 4587536 | tf_op jit(solution)/shard_map/rn,rlk->nlk/dot_general | solution.py:68
  235.4 3.1 copy.65
  238.5 0.0 copy-start.1
  238.5 0.0 reduce-scatter.2.cloned.1.call-update
  238.5 1.2 copy-done.1
  239.7 2.6 fusion.13
  242.3 0.3 copy.55
  242.6 1.0 reshape.85
  243.6 3.0 fusion.14
  246.7 0.3 copy.59
  247.0 1.0 reshape.86
  248.0 58.8 %reduce-scatter.2.cloned.1.call-done = bf16[1,2,64,896]{3,2,0,1:T(8,128)(2,1)} async-done(((bf16[1,32,64,896]{3,2,0,1:T(8,128)(2,1)}), bf16[1,2,64,896]{3,2,0,1:T(8,128)(2,1)}) %reduce-scatter.2.cloned.1.call-update) | async-done | bytes 229392 | tf_op jit(solution)/shard_map/reduce_scatter | solution.py:70
  306.9 1.7 bitcast_convert_fusion
  (3 shorter events, 0.0 us)
Async XLA Ops:
  7.2 49.7 %all-gather.3.cloned.1.call-start = ((), (), s32[]{:S(2)}) async-start(), calls=%async_computation.1 | async-start | bytes 3899392 | tf_op jit(solution)/shard_map/all_gather | solution.py:29
  7.9 192.7 %all-gather.5.cloned.1.call-start = ((), (), s32[]{:S(2)}) async-start(), calls=%async_computation.2 | async-start | bytes 7569408 | tf_op jit(solution)/shard_map/all_gather | solution.py:31
  8.6 298.2 %reduce-scatter.2.cloned.1.call-start = ((), (), s32[]{:S(2)}) async-start(), calls=%async_computation.3 | async-start | bytes 3899392 | tf_op jit(solution)/shard_map/reduce_scatter | solution.py:70
  207.9 8.3 %copy-start = (bf16[2,128,2048]{1,2,0:T(8,128)(2,1)}, bf16[2,128,2048]{1,2,0:T(8,128)(2,1)S(1)}, u32[]{:S(2)}) copy-start(bf16[2,128,2048]{1,2,0:T(8,128)(2,1)S(1)} %copy.71) | copy-start | bytes 3145732
  210.3 1.1 copy-start.2
  238.5 1.2 copy-start.1
Sparse Core Ops, SparseCore 0:
  10.1 46.6 all-gather.2
  59.9 140.6 all-gather.4
  238.6 68.2 reduce-scatter.1
where the time goes:
time: 316 us; the launch traced here: 315 us
  waiting for transfers between devices  246 us (78%)
  matrix products  28.7 us (9%)
  local copies, waits for them, and re-layouts  22.6 us (7%)
  between operations  13.9 us (4%)
  other arithmetic  4.12 us (1%)
    all_gather x1, waiting for transfers between devices, per_device(): whole_weight = lax.all_gather(kv_weight, 'dp', axis=1, tiled=True)  141 us
    reduce_scatter x1, waiting for transfers between devices, per_device(): lax.psum_scatter(rounded.astype(jnp.float32)[None].astype(jnp.bfloat16),...  58.8 us
    all_gather x1, waiting for transfers between devices, per_device(): pool_rows = lax.all_gather(encoded, 'seq', axis=1, tiled=True)[0]  44.6 us
    unnamed x10, local copies, waits for them, and re-layouts  7.21 us
  transfers between devices with their start and end apart: 3, of which 3 were waited for; matrix products, arithmetic and copies ran while one was open for 5% of the time, Pallas kernels for 0%

commit v1 on v0

v1 whole, which is shorter than its diff:
```python
import jax
import jax.numpy as jnp
from jax import lax
from jax.experimental import pallas as pl
from jax.experimental.pallas import tpu as pltpu
from jax.sharding import PartitionSpec as P

MESH = pl.DeviceIdType.MESH
BF = jnp.bfloat16
F32 = jnp.float32

HS = 128
HEADS = 16
SPAN = 64
NLEN = 64
DE = 896
NSH = 32
NSEQ = 16
HALF = DE // 2
QTR = HALF // 2
SCALE = HS ** -0.5


class Sems:
    def __init__(self):
        self.at = {}

    def __call__(self, *name):
        return self.at.setdefault(name, len(self.at))


def nt(a, b):
    return lax.dot_general(a, b, (((1,), (1,)), ((), ())), preferred_element_type=F32)


def tn(a, b):
    return lax.dot_general(a, b, (((0,), (0,)), ((), ())), preferred_element_type=F32)


def nn(a, b):
    return lax.dot_general(a, b, (((1,), (0,)), ((), ())), preferred_element_type=F32)


NSEM = 176


def kernel(
    q_hbm, g_hbm, enc_hbm, w_hbm, ids_s, slot_s, ids_hbm,
    att_hbm, dq_hbm, ge_hbm,
    wbuf, encbuf, qg, qgw, xrd, pbuf, dsbuf, acc, own16, sib16,
    xsend, xrecv, zsend, zrecv, gout, attv, dqv, px, sibids_v, sibids_s,
    ssem, rsem, lsem,
):
    dp = lax.axis_index("dp")
    sq = lax.axis_index("seq")
    y, k = dp // 4, dp % 4
    x, zl, c = sq // 4, (sq // 2) % 2, sq % 2
    o = 2 * zl - 1
    right_y = (((y + 1) % 8) * 4 + k, sq)
    left_y = (((y + 7) % 8) * 4 + k, sq)
    sq_in = sq + 2 - 4 * zl
    outer = (y * 4 + (k + o + 4) % 4, sq_in)
    inner = (dp, sq_in)
    right_x = (dp, (sq + 4) % NSEQ)
    left_x = (dp, (sq + 12) % NSEQ)
    sib = (dp, sq + 1 - 2 * c)
    sem = Sems()
    sent = {0: [], 1: [], 2: []}

    def send(who, name, src, dst, dev):
        i = sem(*name)
        pltpu.make_async_remote_copy(src, dst, ssem.at[i], rsem.at[i], device_id=dev, device_id_type=MESH).start()
        sent[who].append((i, src, dev))

    def recv(name, dst, dev):
        i = sem(*name)
        pltpu.make_async_remote_copy(dst, dst, ssem.at[i], rsem.at[i], device_id=dev, device_id_type=MESH).wait_recv()

    loads = [
        pltpu.make_async_copy(w_hbm, wbuf.at[dp], lsem.at[0]),
        pltpu.make_async_copy(enc_hbm, encbuf.at[sq], lsem.at[1]),
        pltpu.make_async_copy(q_hbm, qg.at[0], lsem.at[2]),
        pltpu.make_async_copy(g_hbm, qg.at[1], lsem.at[3]),
    ]
    for cp in loads:
        cp.start()
    barrier = pltpu.get_barrier_semaphore()
    for dev in (right_y, left_y, outer, inner, right_x, left_x, sib):
        pl.semaphore_signal(barrier, inc=1, device_id=dev, device_id_type=MESH)
    loads[0].wait()
    loads[1].wait()
    pl.semaphore_wait(barrier, 7)

    def shard(dy, kk):
        return ((y + dy + 8) % 8) * 4 + (kk + 8) % 4

    def seq_of(dx, zz):
        return ((x + dx + 4) % 4) * 4 + zz * 2 + c

    def enc_start():
        mine = encbuf.at[sq]
        send(2, ("ea", "r"), mine, mine, right_x)
        send(2, ("ea", "l"), mine, mine, left_x)
        send(2, ("ez",), mine, mine, inner)
        send(2, ("es", 0), mine, mine, sib)
        send(2, ("ids",), ids_hbm, sibids_v, sib)

    def enc_z():
        ref = encbuf.at[seq_of(0, 1 - zl)]
        recv(("ez",), ref, inner)
        send(2, ("eb", "r"), ref, ref, right_x)
        send(2, ("eb", "l"), ref, ref, left_x)
        send(2, ("es", 1), ref, ref, sib)

    def enc_1():
        ref = encbuf.at[seq_of(-1, zl)]
        recv(("ea", "r"), ref, left_x)
        send(2, ("e2", "r"), ref, ref, right_x)
        send(2, ("es", 2), ref, ref, sib)
        ref = encbuf.at[seq_of(1, zl)]
        recv(("ea", "l"), ref, right_x)
        send(2, ("es", 3), ref, ref, sib)

    def enc_2():
        ref = encbuf.at[seq_of(1, 1 - zl)]
        recv(("eb", "l"), ref, right_x)
        send(2, ("e2", "l"), ref, ref, left_x)
        send(2, ("es", 4), ref, ref, sib)
        ref = encbuf.at[seq_of(-1, 1 - zl)]
        recv(("eb", "r"), ref, left_x)
        send(2, ("es", 5), ref, ref, sib)

    def enc_3():
        ref = encbuf.at[seq_of(2, zl)]
        recv(("e2", "r"), ref, left_x)
        send(2, ("es", 6), ref, ref, sib)
        ref = encbuf.at[seq_of(2, 1 - zl)]
        recv(("e2", "l"), ref, right_x)
        send(2, ("es", 7), ref, ref, sib)

    def enc_sib():
        cs = 1 - c
        for i, (dx, zz) in enumerate(((0, zl), (0, 1 - zl), (-1, zl), (1, zl), (1, 1 - zl), (-1, 1 - zl), (2, zl), (2, 1 - zl))):
            recv(("es", i), encbuf.at[((x + dx + 4) % 4) * 4 + zz * 2 + cs], sib)

    OFFS = (0, -1, 1, -2, 2, -3, 3, 4)

    def wp(d, r0=0, n=HALF, core=0):
        return wbuf.at[d, pl.ds(core * HALF + r0, n)]

    def to_sib(core, dy, kk, tag):
        ref = wp(shard(dy, kk), core=core)
        send(core, ("ws", core, dy, tag), ref, ref, sib)

    def core0(n):
        if n < 8:
            dy = OFFS[n]
            d = shard(dy, k)
            if dy == 0:
                send(0, ("yr", 1), wp(d), wp(d), right_y)
                send(0, ("yl", 1), wp(d), wp(d), left_y)
            elif dy == 4:
                recv(("yr", 4), wp(d, 0, QTR), left_y)
                recv(("yl", 4), wp(d, QTR, QTR), right_y)
            elif dy < 0:
                recv(("yr", -dy), wp(d), left_y)
                part = (0, HALF) if dy > -3 else (0, QTR)
                send(0, ("yr", 1 - dy), wp(d, *part), wp(d, *part), right_y)
            else:
                recv(("yl", dy), wp(d), right_y)
                part = (0, HALF) if dy < 3 else (QTR, QTR)
                send(0, ("yl", 1 + dy), wp(d, *part), wp(d, *part), left_y)
            send(0, ("zo", dy), wp(d), wp(d), outer)
            if dy != 0:
                to_sib(0, dy, k, 0)
        if 1 <= n < 9:
            dy = OFFS[n - 1]
            d = shard(dy, k + o)
            recv(("zo", dy), wp(d), outer)
            send(0, ("zi", dy), wp(d), wp(d), inner)
            to_sib(0, dy, k + o, 1)
        if 2 <= n < 10:
            dy = OFFS[n - 2]
            d = shard(dy, k - o)
            recv(("zi", dy), wp(d), inner)
            part = pl.multiple_of((1 - zl) * QTR, QTR)
            send(0, ("zoh", dy), wp(d, part, QTR), wp(d, part, QTR), outer)
            to_sib(0, dy, k - o, 2)
        if 3 <= n < 11:
            dy = OFFS[n - 3]
            d = shard(dy, k + 2)
            part = pl.multiple_of(zl * QTR, QTR)
            recv(("zoh", dy), wp(d, part, QTR), outer)
            send(0, ("zih", dy), wp(d, part, QTR), wp(d, part, QTR), inner)
        if 4 <= n < 12:
            dy = OFFS[n - 4]
            d = shard(dy, k + 2)
            part = pl.multiple_of((1 - zl) * QTR, QTR)
            recv(("zih", dy), wp(d, part, QTR), inner)
            to_sib(0, dy, k + 2, 3)

    def w1(d, r0=0, n=HALF):
        return wp(d, r0, n, core=1)

    KK = (lambda: k, lambda: k + o, lambda: k - o, lambda: k + 2)

    def c1_y(m):
        d = shard(0, KK[m]())
        send(1, ("cr", 1, m), w1(d), w1(d), right_y)
        send(1, ("cl", 1, m), w1(d), w1(d), left_y)
        if m:
            to_sib(1, 0, KK[m](), m)

    def c1_step(s, m):
        kk = KK[m]()
        if s < 4:
            d = shard(-s, kk)
            recv(("cr", s, m), w1(d), left_y)
            part = (0, HALF) if s < 3 else (0, QTR)
            send(1, ("cr", s + 1, m), w1(d, *part), w1(d, *part), right_y)
            to_sib(1, -s, kk, m)
            d = shard(s, kk)
            recv(("cl", s, m), w1(d), right_y)
            part = (0, HALF) if s < 3 else (QTR, QTR)
            send(1, ("cl", s + 1, m), w1(d, *part), w1(d, *part), left_y)
            to_sib(1, s, kk, m)
        else:
            d = shard(4, kk)
            recv(("cr", 4, m), w1(d, 0, QTR), left_y)
            recv(("cl", 4, m), w1(d, QTR, QTR), right_y)
            to_sib(1, 4, kk, m)

    def core1(n):
        if n == 0:
            d = shard(0, k)
            send(1, ("dzo",), w1(d), w1(d), outer)
            c1_y(0)
        elif n == 1:
            d = shard(0, k + o)
            recv(("dzo",), w1(d), outer)
            send(1, ("dzi",), w1(d), w1(d), inner)
            c1_y(1)
            c1_step(1, 0)
        elif n == 2:
            d = shard(0, k - o)
            recv(("dzi",), w1(d), inner)
            part = pl.multiple_of((1 - zl) * QTR, QTR)
            send(1, ("dzoh",), w1(d, part, QTR), w1(d, part, QTR), outer)
            c1_y(2)
            c1_step(1, 1)
        elif n == 3:
            d = shard(0, k + 2)
            part = pl.multiple_of(zl * QTR, QTR)
            recv(("dzoh",), w1(d, part, QTR), outer)
            send(1, ("dzih",), w1(d, part, QTR), w1(d, part, QTR), inner)
            part = pl.multiple_of((1 - zl) * QTR, QTR)
            recv(("dzih",), w1(d, part, QTR), inner)
            c1_y(3)
            c1_step(1, 2)
        else:
            for s, m in {4: ((1, 3), (2, 0)), 5: ((2, 1), (2, 2)), 6: ((2, 3), (3, 0)), 7: ((3, 1), (3, 2)),
                         8: ((3, 3), (4, 0)), 9: ((4, 1), (4, 2)), 10: ((4, 3),), 11: ()}[n]:
                c1_step(s, m)

    def stage(n):
        @pl.when(c == 0)
        def _():
            core0(n)

        @pl.when(c == 1)
        def _():
            core1(n)

    def from_sib(dys):
        @pl.when(c == 0)
        def _():
            for dy in dys:
                for m in range(4):
                    if dy or m:
                        recv(("ws", 1, dy, m), w1(shard(dy, KK[m]())), sib)

        @pl.when(c == 1)
        def _():
            for dy in dys:
                for m in range(4):
                    if dy or m:
                        recv(("ws", 0, dy, m), wp(shard(dy, KK[m]())), sib)

    def project(dy):
        base = ((y + dy + 8) % 8) * 4

        def one(i, _):
            d = base + i
            t = d // HEADS
            h = d % HEADS
            lhs = qg[t, :, pl.ds(pl.multiple_of(h * HS, HS), HS)]
            qgw[d] = nt(lhs, wbuf[d]).astype(BF)
            return 0

        lax.fori_loop(0, 4, one, 0)

    def attend(dy, first):
        g = (y + dy + 8) % 4

        def one(s, _):
            rows = pl.ds(pl.multiple_of(s * SPAN, SPAN), SPAN)
            xs = xrd[s]
            qw = qgw[pl.ds(g * 4, 4), rows, :].reshape(4 * SPAN, DE)
            gw = qgw[pl.ds(HEADS + g * 4, 4), rows, :].reshape(4 * SPAN, DE)
            e = jnp.exp(nt(qw, xs) * SCALE)
            probs = e / jnp.sum(e, axis=-1, keepdims=True)
            d_probs = nt(gw, xs)
            delta = jnp.sum(probs * d_probs, axis=-1, keepdims=True)
            ds = (probs * (d_probs - delta) * SCALE).astype(BF)
            pb = probs.astype(BF)
            pbuf[s, pl.ds(g * 4, 4)] = pb.reshape(4, SPAN, HS)
            dsbuf[s, pl.ds(g * 4, 4)] = ds.reshape(4, SPAN, HS)
            new = tn(ds, qw) + tn(pb, gw)
            if first:
                acc[s] = new
            else:
                acc[s] = acc[s] + new
            return 0

        lax.fori_loop(0, 2, one, 0)

    def outputs(g):
        for t, buf, out in ((0, dsbuf, dqv), (1, pbuf, attv)):
            for s in range(2):
                lhs = buf[s, pl.ds(g * 4, 4)].reshape(4 * SPAN, HS)
                px[:, s] = nn(lhs, xrd[s]).astype(BF).reshape(4, SPAN, DE)
            for i in range(4):
                h = g * 4 + i
                res = nn(px[i].reshape(2 * SPAN, DE), wbuf[t * HEADS + h])
                out[:, h * HS:(h + 1) * HS] = res.astype(BF)

    enc_start()
    stage(0)
    enc_z()
    stage(1)
    enc_1()
    stage(2)
    enc_2()
    stage(3)
    loads[2].wait()
    loads[3].wait()
    project_0_done = False
    enc_3()
    stage(4)
    stage(5)
    from_sib((0,))
    project(0)
    stage(6)
    enc_sib()
    pos = [slot_s[0, ids_s[0, s, r]] for s in range(2) for r in range(2)]
    for s in range(2):
        for r in range(2):
            p = pos[2 * s + r]
            xrd[s, r * NLEN:(r + 1) * NLEN] = encbuf[p // 2, p % 2]
    recv(("ids",), sibids_v, sib)
    cp = pltpu.make_async_copy(sibids_v, sibids_s, lsem.at[4])
    cp.start()
    cp.wait()
    stage(7)
    from_sib((-1, 1))
    project(-1)
    project(1)
    stage(8)
    from_sib((-2, 2))
    project(-2)
    stage(9)
    project(2)
    attend(2, True)
    stage(10)
    from_sib((-3, 3))
    project(-3)
    stage(11)
    project(3)
    attend(1, False)
    attend(-1, False)
    from_sib((4,))
    project(4)
    attend(0, False)

    for s in range(2):
        own16[s, 0:2] = acc[s].astype(BF).reshape(2, NLEN, DE)
        own16[s, 2] = jnp.zeros((NLEN, DE), BF)
        sib16[s, 2] = jnp.zeros((NLEN, DE), BF)
    send(2, ("rs",), own16.at[:, 0:2], sib16.at[:, 0:2], sib)
    spos = [slot_s[0, sibids_s[0, s * 2 + r]] for s in range(2) for r in range(2)]

    def which(ps, s, p):
        return jnp.where(ps[2 * s] == p, 0, jnp.where(ps[2 * s + 1] == p, 1, 2))

    def chip_sum(dx, zz, j, rows):
        p = ((x + dx + 4) % 4) * 8 + zz * 4 + 2 * c + j
        total = own16[0, which(pos, 0, p), rows].astype(F32) + own16[1, which(pos, 1, p), rows].astype(F32)
        return total + (sib16[0, which(spos, 0, p), rows].astype(F32) + sib16[1, which(spos, 1, p), rows].astype(F32))

    TOP, BOT = slice(0, 32), slice(32, 64)
    DIRS = (("r", right_x, left_x, 1, TOP, BOT), ("l", left_x, right_x, -1, BOT, TOP))

    def far(half):
        for di, (nm, to, _, sg, mine, _) in enumerate(DIRS):
            m = 0 if half == 0 else 1
            zz = 1 - zl if half == 0 else zl
            for j in range(2):
                xsend[di, m, j] = chip_sum(2, zz, j, mine).astype(BF)
            send(2, ("x", m, nm), xsend.at[di, m], xrecv.at[di, m], to)

    def near(half):
        for di, (nm, to, _, sg, _, other) in enumerate(DIRS):
            m = 2 if half == 0 else 4
            zz = 1 - zl if half == 0 else zl
            for j in range(2):
                xsend[di, m, j] = chip_sum(sg, zz, j, other).astype(BF)
            send(2, ("x", m, nm), xsend.at[di, m], xrecv.at[di, m], to)

    def near_add(half):
        for di, (nm, to, frm, sg, mine, _) in enumerate(DIRS):
            m = 3 if half == 0 else 5
            zz = 1 - zl if half == 0 else zl
            recv(("x", half, nm), xrecv.at[di, half], frm)
            for j in range(2):
                xsend[di, m, j] = (chip_sum(sg, zz, j, mine) + xrecv[di, half, j].astype(F32)).astype(BF)
            send(2, ("x", m, nm), xsend.at[di, m], xrecv.at[di, m], to)

    def total(half):
        a, b = (2, 3) if half == 0 else (4, 5)
        for di, (nm, _, frm, _, _, _) in enumerate(DIRS):
            for m in (a, b):
                recv(("x", m, nm), xrecv.at[di, m], frm)
        zz = 1 - zl if half == 0 else zl
        for j in range(2):
            top = chip_sum(0, zz, j, TOP) + xrecv[0, b, j].astype(F32) + xrecv[1, a, j].astype(F32)
            bot = chip_sum(0, zz, j, BOT) + xrecv[0, a, j].astype(F32) + xrecv[1, b, j].astype(F32)
            if half == 0:
                zsend[j, TOP] = top.astype(BF)
                zsend[j, BOT] = bot.astype(BF)
            else:
                gout[j, TOP] = top
                gout[j, BOT] = bot

    recv(("rs",), sib16.at[:, 0:2], sib)
    far(0)
    far(1)
    near(0)
    outputs(0)
    near_add(0)
    near(1)
    outputs(1)
    near_add(1)
    outputs(2)
    total(0)
    send(2, ("rz",), zsend, zrecv, inner)
    outputs(3)
    stores = [
        pltpu.make_async_copy(attv, att_hbm, lsem.at[5]),
        pltpu.make_async_copy(dqv, dq_hbm, lsem.at[6]),
    ]
    for cp in stores:
        cp.start()
    total(1)
    recv(("rz",), zrecv, inner)
    for j in range(2):
        gout[j] = gout[j] + zrecv[j].astype(F32)
    stores.append(pltpu.make_async_copy(gout, ge_hbm, lsem.at[7]))
    stores[-1].start()

    def drain(items):
        for i, src, dev in items:
            pltpu.make_async_remote_copy(src, src, ssem.at[i], rsem.at[i], device_id=dev, device_id_type=MESH).wait_send()

    drain(sent[2])

    @pl.when(c == 0)
    def _():
        drain([(i, src_like(wbuf, n), dev) for i, n, dev in plain(sent[0])])

    @pl.when(c == 1)
    def _():
        drain([(i, src_like(wbuf, n), dev) for i, n, dev in plain(sent[1])])

    for cp in stores:
        cp.wait()
    assert len(sem.at) <= NSEM, len(sem.at)


def plain(items):
    return [(i, src.shape[0], dev) for i, src, dev in items]


def src_like(wbuf, rows):
    return wbuf.at[0, pl.ds(0, rows)]


def per_device(queries, grad_out, encoded, kv_weight, neighbour_ids, slot_map):
    ids_pad = jnp.zeros((8, 128), jnp.int32).at[0, 0:4].set(neighbour_ids.reshape(4))
    anyspec = pl.BlockSpec(memory_space=pl.ANY)
    smem = pl.BlockSpec(memory_space=pltpu.SMEM)
    att, dq, ge = pl.pallas_call(
        kernel,
        out_shape=(
            jax.ShapeDtypeStruct((2 * SPAN, HEADS * HS), BF),
            jax.ShapeDtypeStruct((2 * SPAN, HEADS * HS), BF),
            jax.ShapeDtypeStruct((2, NLEN, DE), F32),
        ),
        in_specs=[anyspec, anyspec, anyspec, anyspec, smem, smem, anyspec],
        out_specs=(anyspec, anyspec, anyspec),
        scratch_shapes=[
            pltpu.VMEM((NSH, DE, HS), BF),
            pltpu.VMEM((NSEQ, 2, NLEN, DE), BF),
            pltpu.VMEM((2, 2 * SPAN, HEADS * HS), BF),
            pltpu.VMEM((NSH, 2 * SPAN, DE), BF),
            pltpu.VMEM((2, 2 * NLEN, DE), BF),
            pltpu.VMEM((2, HEADS, SPAN, HS), BF),
            pltpu.VMEM((2, HEADS, SPAN, HS), BF),
            pltpu.VMEM((2, 2 * NLEN, DE), F32),
            pltpu.VMEM((2, 3, NLEN, DE), BF),
            pltpu.VMEM((2, 3, NLEN, DE), BF),
            pltpu.VMEM((2, 6, 2, 32, DE), BF),
            pltpu.VMEM((2, 6, 2, 32, DE), BF),
            pltpu.VMEM((2, NLEN, DE), BF),
            pltpu.VMEM((2, NLEN, DE), BF),
            pltpu.VMEM((2, NLEN, DE), F32),
            pltpu.VMEM((2 * SPAN, HEADS * HS), BF),
            pltpu.VMEM((2 * SPAN, HEADS * HS), BF),
            pltpu.VMEM((4, 2, SPAN, DE), BF),
            pltpu.VMEM((8, 128), jnp.int32),
            pltpu.SMEM((8, 128), jnp.int32),
            pltpu.SemaphoreType.DMA((NSEM,)),
            pltpu.SemaphoreType.DMA((NSEM,)),
            pltpu.SemaphoreType.DMA((8,)),
        ],
        compiler_params=pltpu.CompilerParams(
            collective_id=0, has_side_effects=True, vmem_limit_bytes=56 * 1024 * 1024
        ),
    )(queries[0], grad_out[0], encoded[0], kv_weight, neighbour_ids, slot_map, ids_pad)
    return att[None], dq[None], ge[None]


def solution(mesh):
    in_specs = (
        P("dp", "seq", None),
        P("dp", "seq", None),
        P("dp", "seq", None, None),
        P(None, "dp"),
        P("dp", "seq", None),
        P("dp", None),
    )
    out_specs = (P("dp", "seq", None), P("dp", "seq", None), P("dp", "seq", None, None))
    return jax.shard_map(
        per_device, mesh=mesh, in_specs=in_specs, out_specs=out_specs, check_vma=False
    )
```

time: 316 us -> 93 us (0.29)
  the two profiles are of different devices: /device:TPU:16 before, /device:TPU:27 now
where the time goes in v1:
time: 93 us; the launch traced here: 92.7 us
  Pallas kernels  86.8 us (93%)
  local copies, waits for them, and re-layouts  5.27 us (6%)
    pallas_call x1, Pallas kernels, per_device(): pl.pallas_call(kernel, out_shape=(jax.ShapeDtypeStruct((2 * SPAN, HEADS *...  86.8 us
    unnamed x9, local copies, waits for them, and re-layouts  4.59 us

profile of v1, /device:TPU:27, one launch (start us, length us, event | category | flops | bytes accessed | tf_op | source)
XLA Modules:
  0.0 92.7 jit_solution(4866994318140218463)
XLA Ops:
  0.6 0.0 copy-start.2
  0.6 0.7 copy-done.2
  1.3 0.1 reshape.39
  1.4 0.6 scatter.4.ids_hbm
  2.0 86.8 %shard_map.85 = (bf16[128,2048]{1,0:T(8,128)(2,1)}, bf16[128,2048]{1,0:T(8,128)(2,1)}, f32[2,64,896]{2,1,0:T(8,128)}) custom-call(bf16[128,2048]{1,0:T(8,128)(2,1)} %bitcast.6, bf16[128,2048]{1,0:T(8,128)(2,1)} %bitcast.7, bf16[2,64,896]{2,1,0:T(8,128)(2,1)} %bitcast.11, bf16[896,128]{1,0:T(8,128)(2,1)} %w_hbm.1, s32[1,2,2]{2,1,0:T(2,128)} %ids_s.1, ...), custom_call_target="tpu_custom_call" | custom-call | tf_op jit(solution)/shard_map/pallas_call | solution.py:501
  88.8 0.0 copy-start
  88.8 1.9 %copy.12 = bf16[1,128,2048]{2,1,0:T(8,128)(2,1)} copy(bf16[1,128,2048]{2,1,0:T(8,128)(2,1)} %bitcast.9) | data formatting | bytes 1048576
  90.7 0.0 copy-done
  90.7 0.0 copy-start.1
  90.7 0.8 copy.13
  91.5 0.4 copy-done.1
  92.0 0.8 copy.14
Async XLA Ops:
  0.6 0.7 copy-start.2
  88.8 2.0 %copy-start = (bf16[128,2048]{1,0:T(8,128)(2,1)S(1)}, bf16[128,2048]{1,0:T(8,128)(2,1)}, u32[]{:S(2)}) copy-start(bf16[128,2048]{1,0:T(8,128)(2,1)} %get-tuple-element.19) | copy-start | bytes 1572868
  90.7 1.2 %copy-start.1 = (f32[2,64,896]{2,1,0:T(8,128)S(1)}, f32[2,64,896]{2,1,0:T(8,128)}, u32[]{:S(2)}) copy-start(f32[2,64,896]{2,1,0:T(8,128)} %get-tuple-element.20) | copy-start | bytes 1376260

commit v2 on v1

v2 whole, which is shorter than its diff:
```python
import jax
import jax.numpy as jnp
from jax import lax
from jax.experimental import pallas as pl
from jax.experimental.pallas import tpu as pltpu
from jax.sharding import PartitionSpec as P

MESH = pl.DeviceIdType.MESH
BF = jnp.bfloat16
F32 = jnp.float32

HS = 128
HEADS = 16
SPAN = 64
NLEN = 64
DE = 896
NSH = 32
NSEQ = 16
CUT = 416
SCALE = HS ** -0.5


class Sems:
    def __init__(self):
        self.at = {}

    def __call__(self, *name):
        return self.at.setdefault(name, len(self.at))


def nt(a, b):
    return lax.dot_general(a, b, (((1,), (1,)), ((), ())), preferred_element_type=F32)


def tn(a, b):
    return lax.dot_general(a, b, (((0,), (0,)), ((), ())), preferred_element_type=F32)


def nn(a, b):
    return lax.dot_general(a, b, (((1,), (0,)), ((), ())), preferred_element_type=F32)


NSEM = 192


def kernel(
    q_hbm, g_hbm, enc_hbm, w_hbm, ids_s, slot_s,
    attv, dqv, gout,
    wbuf, encbuf, qg, qgw, xrd, pbuf, dsbuf, acc, own16, sib16,
    xsend, xrecv, zsend, zrecv, px, ids_v, sibids_v, sibids_s,
    ssem, rsem, lsem,
):
    dp = lax.axis_index("dp")
    sq = lax.axis_index("seq")
    y, k = dp // 4, dp % 4
    x, zl, c = sq // 4, (sq // 2) % 2, sq % 2
    o = 2 * zl - 1
    right2_y = (((y + 2) % 8) * 4 + k, sq)
    left2_y = (((y + 6) % 8) * 4 + k, sq)
    right_y = (((y + 1) % 8) * 4 + k, sq)
    left_y = (((y + 7) % 8) * 4 + k, sq)
    sq_in = sq + 2 - 4 * zl
    outer = (y * 4 + (k + o + 4) % 4, sq_in)
    out_pair = (y * 4 + (k + o + 4) % 4, sq)
    in_pair = (y * 4 + (k - o + 4) % 4, sq)
    far = (y * 4 + (k + 2) % 4, sq_in)
    inner = (dp, sq_in)
    right_x = (dp, (sq + 4) % NSEQ)
    left_x = (dp, (sq + 12) % NSEQ)
    sib = (dp, sq + 1 - 2 * c)
    sem = Sems()
    sent = {0: [], 1: [], 2: []}

    def send(who, name, src, dst, dev):
        i = sem(*name)
        pltpu.make_async_remote_copy(src, dst, ssem.at[i], rsem.at[i], device_id=dev, device_id_type=MESH).start()
        sent[who].append((i, src, dev))

    def recv(name, dst, dev):
        i = sem(*name)
        pltpu.make_async_remote_copy(dst, dst, ssem.at[i], rsem.at[i], device_id=dev, device_id_type=MESH).wait_recv()

    loads = [
        pltpu.make_async_copy(w_hbm, wbuf.at[dp], lsem.at[0]),
        pltpu.make_async_copy(enc_hbm, encbuf.at[sq], lsem.at[1]),
        pltpu.make_async_copy(q_hbm, qg.at[0], lsem.at[2]),
        pltpu.make_async_copy(g_hbm, qg.at[1], lsem.at[3]),
    ]
    for cp in loads:
        cp.start()
    barrier = pltpu.get_barrier_semaphore()
    for dev in (right_y, left_y, right2_y, left2_y, outer, far, out_pair, in_pair, inner, right_x, left_x, sib):
        pl.semaphore_signal(barrier, inc=1, device_id=dev, device_id_type=MESH)
    lane = lax.broadcasted_iota(jnp.int32, (8, 128), 1)
    ids_vec = jnp.zeros((8, 128), jnp.int32)
    for i in range(4):
        ids_vec = jnp.where(lane == i, ids_s[0, i // 2, i % 2], ids_vec)
    ids_v[...] = ids_vec
    pl.semaphore_wait(barrier, 12)

    def shard(dy, kk):
        return ((y + dy + 8) % 8) * 4 + (kk + 8) % 4

    def seq_of(dx, zz):
        return ((x + dx + 4) % 4) * 4 + zz * 2 + c

    def enc_start():
        mine = encbuf.at[sq]
        send(2, ("ez",), enc_hbm, mine, inner)
        send(2, ("ea", "r"), enc_hbm, mine, right_x)
        send(2, ("ea", "l"), enc_hbm, mine, left_x)
        send(2, ("es", 0), enc_hbm, mine, sib)
        send(2, ("ids",), ids_v, sibids_v, sib)

    def enc_z():
        ref = encbuf.at[seq_of(0, 1 - zl)]
        recv(("ez",), ref, inner)
        send(2, ("eb", "r"), ref, ref, right_x)
        send(2, ("eb", "l"), ref, ref, left_x)
        send(2, ("es", 1), ref, ref, sib)

    def enc_1():
        ref = encbuf.at[seq_of(-1, zl)]
        recv(("ea", "r"), ref, left_x)
        send(2, ("e2", "r"), ref, ref, right_x)
        send(2, ("es", 2), ref, ref, sib)
        ref = encbuf.at[seq_of(1, zl)]
        recv(("ea", "l"), ref, right_x)
        send(2, ("es", 3), ref, ref, sib)

    def enc_2():
        ref = encbuf.at[seq_of(1, 1 - zl)]
        recv(("eb", "l"), ref, right_x)
        send(2, ("e2", "l"), ref, ref, left_x)
        send(2, ("es", 4), ref, ref, sib)
        ref = encbuf.at[seq_of(-1, 1 - zl)]
        recv(("eb", "r"), ref, left_x)
        send(2, ("es", 5), ref, ref, sib)

    def enc_3():
        ref = encbuf.at[seq_of(2, zl)]
        recv(("e2", "r"), ref, left_x)
        send(2, ("es", 6), ref, ref, sib)
        ref = encbuf.at[seq_of(2, 1 - zl)]
        recv(("e2", "l"), ref, right_x)
        send(2, ("es", 7), ref, ref, sib)

    def enc_sib():
        cs = 1 - c
        for i, (dx, zz) in enumerate(((0, zl), (0, 1 - zl), (-1, zl), (1, zl), (1, 1 - zl), (-1, 1 - zl), (2, zl), (2, 1 - zl))):
            recv(("es", i), encbuf.at[((x + dx + 4) % 4) * 4 + zz * 2 + cs], sib)

    R0 = (0, CUT)
    RN = (CUT, DE - CUT)

    def part(core, half=None):
        n = RN[core]
        if half is None:
            return R0[core], n
        return pl.multiple_of(R0[core] + half * (n // 2), 16), n // 2

    def wp(d, core, half=None):
        r0, n = part(core, half)
        return wbuf.at[d, pl.ds(r0, n)]

    def own(core, half=None):
        r0, n = part(core, half)
        return w_hbm.at[pl.ds(r0, n)]

    KK = (lambda: k, lambda: k + o, lambda: k - o, lambda: k + 2)

    def to_sib(core, dy, m):
        ref = wp(shard(dy, KK[m]()), core)
        send(core, ("ws", core, dy, m), ref, ref, sib)

    OFFS = (0, -1, 1, -2, 2, -3, 3, 4)

    def y0(dy):
        d = shard(dy, k)
        mine, dst = own(0), wp(d, 0)
        if dy == 0:
            send(0, ("y2r",), mine, dst, right2_y)
            send(0, ("y2l",), mine, dst, left2_y)
            send(0, ("y1r",), mine, dst, right_y)
            send(0, ("y1l",), mine, dst, left_y)
        elif dy == -1:
            recv(("y1r",), dst, left_y)
        elif dy == 1:
            recv(("y1l",), dst, right_y)
        elif dy == -2:
            recv(("y2r",), dst, left2_y)
            send(0, ("y3r",), dst, dst, right_y)
            send(0, ("y4r",), wp(d, 0, 0), wp(d, 0, 0), right2_y)
        elif dy == 2:
            recv(("y2l",), dst, right2_y)
            send(0, ("y3l",), dst, dst, left_y)
            send(0, ("y4l",), wp(d, 0, 1), wp(d, 0, 1), left2_y)
        elif dy == -3:
            recv(("y3r",), dst, left_y)
        elif dy == 3:
            recv(("y3l",), dst, right_y)
        else:
            recv(("y4r",), wp(d, 0, 0), left2_y)
            recv(("y4l",), wp(d, 0, 1), right2_y)

    def z0_start(dy):
        d = shard(dy, k)
        src = own(0) if dy == 0 else wp(d, 0)
        half = own(0, zl) if dy == 0 else wp(d, 0, zl)
        send(0, ("zo", dy), src, wp(d, 0), outer)
        send(0, ("zf", dy), half, wp(d, 0, zl), far)

    def z0_pass(dy):
        ref = wp(shard(dy, k + o), 0)
        recv(("zo", dy), ref, outer)
        send(0, ("zi", dy), ref, ref, inner)
        to_sib(0, dy, 1)
        ref = wp(shard(dy, k + 2), 0, 1 - zl)
        recv(("zf", dy), ref, far)
        send(0, ("zh", dy), ref, ref, inner)

    def z0_last(dy):
        recv(("zi", dy), wp(shard(dy, k - o), 0), inner)
        to_sib(0, dy, 2)
        recv(("zh", dy), wp(shard(dy, k + 2), 0, zl), inner)
        to_sib(0, dy, 3)

    def core0(n):
        if n < 8:
            dy = OFFS[n]
            y0(dy)
            z0_start(dy)
            if n:
                to_sib(0, dy, 0)
        if 3 <= n <= 10:
            z0_pass(OFFS[n - 3])
        if 5 <= n <= 12:
            z0_last(OFFS[n - 5])

    def y1_start(m):
        d = shard(0, KK[m]())
        src = own(1) if m == 0 else wp(d, 1)
        send(1, ("yr", 1, m), src, wp(d, 1), right_y)
        send(1, ("yl", 1, m), src, wp(d, 1), left_y)

    def y1_pass(dy, m):
        d = shard(dy, KK[m]())
        if dy == 4:
            recv(("yr", 4, m), wp(d, 1, 0), left_y)
            recv(("yl", 4, m), wp(d, 1, 1), right_y)
        else:
            nm, to, frm, half = ("yr", right_y, left_y, 0) if dy < 0 else ("yl", left_y, right_y, 1)
            st = abs(dy)
            recv((nm, st, m), wp(d, 1), frm)
            ref = wp(d, 1) if st < 3 else wp(d, 1, half)
            send(1, (nm, st + 1, m), ref, ref, to)
        to_sib(1, dy, m)

    def both(st, m):
        if st < 4:
            y1_pass(-st, m)
            y1_pass(st, m)
        else:
            y1_pass(4, m)

    def core1(n):
        if n == 0:
            d = shard(0, k)
            send(1, ("wo",), own(1), wp(d, 1), outer)
            send(1, ("wd",), own(1), wp(d, 1), out_pair)
            send(1, ("wf",), own(1), wp(d, 1), far)
            y1_start(0)
        elif n == 2:
            for m, nm, frm in ((1, "wo", outer), (2, "wd", in_pair), (3, "wf", far)):
                recv((nm,), wp(shard(0, KK[m]()), 1), frm)
                y1_start(m)
                to_sib(1, 0, m)
        else:
            for sm in {1: ((1, 0),), 3: ((1, 1), (2, 0)), 4: ((1, 2), (1, 3)), 5: ((2, 1), (3, 0)), 6: ((2, 2), (2, 3)),
                       7: ((3, 1), (4, 0)), 8: ((3, 2), (3, 3)), 9: ((4, 1),), 10: ((4, 2),), 11: ((4, 3),), 12: ()}[n]:
                both(*sm)

    def stage(n):
        @pl.when(c == 0)
        def _():
            core0(n)

        @pl.when(c == 1)
        def _():
            core1(n)

    def from_sib(dys):
        for core in range(2):
            @pl.when(c == core)
            def _():
                for dy in dys:
                    for m in range(4):
                        if dy or m:
                            recv(("ws", 1 - core, dy, m), wp(shard(dy, KK[m]()), 1 - core), sib)

    def project(dy):
        base = ((y + dy + 8) % 8) * 4

        def one(i, _):
            d = base + i
            t = d // HEADS
            h = d % HEADS
            lhs = qg[t, :, pl.ds(pl.multiple_of(h * HS, HS), HS)]
            qgw[d] = nt(lhs, wbuf[d]).astype(BF)
            return 0

        lax.fori_loop(0, 4, one, 0, unroll=True)

    def attend(dy, first):
        g = (y + dy + 8) % 4

        def one(s, _):
            rows = pl.ds(pl.multiple_of(s * SPAN, SPAN), SPAN)
            xs = xrd[s]
            qw = qgw[pl.ds(g * 4, 4), rows, :].reshape(4 * SPAN, DE)
            gw = qgw[pl.ds(HEADS + g * 4, 4), rows, :].reshape(4 * SPAN, DE)
            e = jnp.exp(nt(qw, xs) * SCALE)
            probs = e / jnp.sum(e, axis=-1, keepdims=True)
            d_probs = nt(gw, xs)
            delta = jnp.sum(probs * d_probs, axis=-1, keepdims=True)
            ds = (probs * (d_probs - delta) * SCALE).astype(BF)
            pb = probs.astype(BF)
            pbuf[s, pl.ds(g * 4, 4)] = pb.reshape(4, SPAN, HS)
            dsbuf[s, pl.ds(g * 4, 4)] = ds.reshape(4, SPAN, HS)
            new = tn(ds, qw) + tn(pb, gw)
            if first:
                acc[s] = new
            else:
                acc[s] = acc[s] + new
            return 0

        lax.fori_loop(0, 2, one, 0, unroll=True)

    def outputs(dy):
        g = (y + dy + 8) % 4
        for t, buf, out in ((0, dsbuf, dqv), (1, pbuf, attv)):
            for s in range(2):
                lhs = buf[s, pl.ds(g * 4, 4)].reshape(4 * SPAN, HS)
                px[t, :, s] = nn(lhs, xrd[s]).astype(BF).reshape(4, SPAN, DE)
            for i in range(4):
                h = g * 4 + i
                res = nn(px[t, i].reshape(2 * SPAN, DE), wbuf[t * HEADS + h])
                out[:, pl.ds(pl.multiple_of(h * HS, HS), HS)] = res.astype(BF)

    enc_start()
    stage(0)
    stage(1)
    stage(2)
    enc_z()
    stage(3)
    enc_1()
    for cp in loads:
        cp.wait()
    stage(4)
    stage(5)
    from_sib((0,))
    project(0)
    stage(6)
    enc_2()
    stage(7)
    from_sib((-1, 1))
    project(-1)
    project(1)
    stage(8)
    enc_3()
    stage(9)
    from_sib((-2, 2))
    project(-2)
    project(2)
    enc_sib()
    pos = [slot_s[0, ids_s[0, s, r]] for s in range(2) for r in range(2)]
    for s in range(2):
        for r in range(2):
            p = pos[2 * s + r]
            xrd[s, r * NLEN:(r + 1) * NLEN] = encbuf[p // 2, p % 2]
    stage(10)
    recv(("ids",), sibids_v, sib)
    cp = pltpu.make_async_copy(sibids_v, sibids_s, lsem.at[4])
    cp.start()
    attend(2, True)
    from_sib((-3,))
    project(-3)
    attend(1, False)
    outputs(2)
    cp.wait()
    stage(11)
    from_sib((3,))
    project(3)
    attend(-1, False)
    stage(12)
    from_sib((4,))
    project(4)
    attend(0, False)

    for s in range(2):
        own16[s, 0:2] = acc[s].astype(BF).reshape(2, NLEN, DE)
        own16[s, 2] = jnp.zeros((NLEN, DE), BF)
        sib16[s, 2] = jnp.zeros((NLEN, DE), BF)
    send(2, ("rs",), own16.at[:, 0:2], sib16.at[:, 0:2], sib)
    spos = [slot_s[0, sibids_s[0, s * 2 + r]] for s in range(2) for r in range(2)]

    def which(ps, s, p):
        return jnp.where(ps[2 * s] == p, 0, jnp.where(ps[2 * s + 1] == p, 1, 2))

    def chip_sum(dx, zz, j, rows):
        p = ((x + dx + 4) % 4) * 8 + zz * 4 + 2 * c + j
        total = own16[0, which(pos, 0, p), rows].astype(F32) + own16[1, which(pos, 1, p), rows].astype(F32)
        return total + (sib16[0, which(spos, 0, p), rows].astype(F32) + sib16[1, which(spos, 1, p), rows].astype(F32))

    TOP, BOT = slice(0, 32), slice(32, 64)
    DIRS = (("r", right_x, left_x, 1, TOP, BOT), ("l", left_x, right_x, -1, BOT, TOP))

    def far(half):
        for di, (nm, to, _, sg, mine, _) in enumerate(DIRS):
            m = 0 if half == 0 else 1
            zz = 1 - zl if half == 0 else zl
            for j in range(2):
                xsend[di, m, j] = chip_sum(2, zz, j, mine).astype(BF)
            send(2, ("x", m, nm), xsend.at[di, m], xrecv.at[di, m], to)

    def near(half):
        for di, (nm, to, _, sg, _, other) in enumerate(DIRS):
            m = 2 if half == 0 else 4
            zz = 1 - zl if half == 0 else zl
            for j in range(2):
                xsend[di, m, j] = chip_sum(sg, zz, j, other).astype(BF)
            send(2, ("x", m, nm), xsend.at[di, m], xrecv.at[di, m], to)

    def near_add(half):
        for di, (nm, to, frm, sg, mine, _) in enumerate(DIRS):
            m = 3 if half == 0 else 5
            zz = 1 - zl if half == 0 else zl
            recv(("x", half, nm), xrecv.at[di, half], frm)
            for j in range(2):
                xsend[di, m, j] = (chip_sum(sg, zz, j, mine) + xrecv[di, half, j].astype(F32)).astype(BF)
            send(2, ("x", m, nm), xsend.at[di, m], xrecv.at[di, m], to)

    def total(half):
        a, b = (2, 3) if half == 0 else (4, 5)
        for di, (nm, _, frm, _, _, _) in enumerate(DIRS):
            for m in (a, b):
                recv(("x", m, nm), xrecv.at[di, m], frm)
        zz = 1 - zl if half == 0 else zl
        for j in range(2):
            top = chip_sum(0, zz, j, TOP) + xrecv[0, b, j].astype(F32) + xrecv[1, a, j].astype(F32)
            bot = chip_sum(0, zz, j, BOT) + xrecv[0, a, j].astype(F32) + xrecv[1, b, j].astype(F32)
            if half == 0:
                zsend[j, TOP] = top.astype(BF)
                zsend[j, BOT] = bot.astype(BF)
            else:
                gout[j, TOP] = top
                gout[j, BOT] = bot

    outputs(1)
    recv(("rs",), sib16.at[:, 0:2], sib)
    far(0)
    near(0)
    far(1)
    outputs(-1)
    near_add(0)
    near(1)
    near_add(1)
    outputs(0)
    total(0)
    send(2, ("rz",), zsend, zrecv, inner)
    total(1)
    recv(("rz",), zrecv, inner)
    for j in range(2):
        gout[j] = gout[j] + zrecv[j].astype(F32)

    def drain(items):
        for i, src, dev in items:
            pltpu.make_async_remote_copy(src, src, ssem.at[i], rsem.at[i], device_id=dev, device_id_type=MESH).wait_send()

    drain(sent[2])
    rows_sent = [[(i, src.shape[0], dev) for i, src, dev in sent[core]] for core in range(2)]

    for core in range(2):
        @pl.when(c == core)
        def _():
            drain([(i, wbuf.at[0, pl.ds(0, n)], dev) for i, n, dev in rows_sent[core]])

    assert len(sem.at) <= NSEM, len(sem.at)


def per_device(queries, grad_out, encoded, kv_weight, neighbour_ids, slot_map):
    anyspec = pl.BlockSpec(memory_space=pltpu.HBM)
    smem = pl.BlockSpec(memory_space=pltpu.SMEM)
    vmem = pl.BlockSpec(memory_space=pltpu.VMEM)
    att, dq, ge = pl.pallas_call(
        kernel,
        out_shape=(
            pltpu.VMEM((2 * SPAN, HEADS * HS), BF),
            pltpu.VMEM((2 * SPAN, HEADS * HS), BF),
            pltpu.VMEM((2, NLEN, DE), F32),
        ),
        in_specs=[anyspec, anyspec, anyspec, anyspec, smem, smem],
        out_specs=(vmem, vmem, vmem),
        scratch_shapes=[
            pltpu.VMEM((NSH, DE, HS), BF),
            pltpu.VMEM((NSEQ, 2, NLEN, DE), BF),
            pltpu.VMEM((2, 2 * SPAN, HEADS * HS), BF),
            pltpu.VMEM((NSH, 2 * SPAN, DE), BF),
            pltpu.VMEM((2, 2 * NLEN, DE), BF),
            pltpu.VMEM((2, HEADS, SPAN, HS), BF),
            pltpu.VMEM((2, HEADS, SPAN, HS), BF),
            pltpu.VMEM((2, 2 * NLEN, DE), F32),
            pltpu.VMEM((2, 3, NLEN, DE), BF),
            pltpu.VMEM((2, 3, NLEN, DE), BF),
            pltpu.VMEM((2, 6, 2, 32, DE), BF),
            pltpu.VMEM((2, 6, 2, 32, DE), BF),
            pltpu.VMEM((2, NLEN, DE), BF),
            pltpu.VMEM((2, NLEN, DE), BF),
            pltpu.VMEM((2, 4, 2, SPAN, DE), BF),
            pltpu.VMEM((8, 128), jnp.int32),
            pltpu.VMEM((8, 128), jnp.int32),
            pltpu.SMEM((8, 128), jnp.int32),
            pltpu.SemaphoreType.DMA((NSEM,)),
            pltpu.SemaphoreType.DMA((NSEM,)),
            pltpu.SemaphoreType.DMA((8,)),
        ],
        compiler_params=pltpu.CompilerParams(
            collective_id=0, has_side_effects=True, vmem_limit_bytes=58 * 1024 * 1024
        ),
    )(queries[0], grad_out[0], encoded[0], kv_weight, neighbour_ids, slot_map)
    return att[None], dq[None], ge[None]


def solution(mesh):
    in_specs = (
        P("dp", "seq", None),
        P("dp", "seq", None),
        P("dp", "seq", None, None),
        P(None, "dp"),
        P("dp", "seq", None),
        P("dp", None),
    )
    out_specs = (P("dp", "seq", None), P("dp", "seq", None), P("dp", "seq", None, None))
    return jax.shard_map(
        per_device, mesh=mesh, in_specs=in_specs, out_specs=out_specs, check_vma=False
    )
```

time: 93 us -> 77.5 us (0.83)
  the two profiles are of different devices: /device:TPU:27 before, /device:TPU:24 now
where the time goes in v2:
time: 77.5 us; the launch traced here: 77.3 us
  Pallas kernels  74.3 us (96%)
  local copies, waits for them, and re-layouts  2.36 us (3%)
    pallas_call x1, Pallas kernels, per_device(): pl.pallas_call(kernel, out_shape=(pltpu.VMEM((2 * SPAN, HEADS * HS), BF),...  74.3 us
    unnamed x3, local copies, waits for them, and re-layouts  2.36 us

profile of v2, /device:TPU:24, one launch (start us, length us, event | category | flops | bytes accessed | tf_op | source)
XLA Modules:
  0.0 77.3 jit_solution(17082152021021539786)
XLA Ops:
  0.6 74.3 %shard_map.85 = (bf16[128,2048]{1,0:T(8,128)(2,1)S(1)}, bf16[128,2048]{1,0:T(8,128)(2,1)S(1)}, f32[2,64,896]{2,1,0:T(8,128)S(1)}) custom-call(bf16[128,2048]{1,0:T(8,128)(2,1)} %bitcast.9, bf16[128,2048]{1,0:T(8,128)(2,1)} %bitcast.10, bf16[2,64,896]{2,1,0:T(8,128)(2,1)} %bitcast.11, bf16[896,128]{1,0:T(8,128)(2,1)} %w_hbm.1, s32[1,2,2]{2,1,0:T(2,128)} %ids_s.1, ...), custom_call_target="tpu_custom_call" | custom-call | tf_op jit(solution)/shard_map/pallas_call | solution.py:495
  75.0 0.8 %copy.12 = bf16[1,128,2048]{2,1,0:T(8,128)(2,1)} copy(bf16[1,128,2048]{2,1,0:T(8,128)(2,1)S(1)} %bitcast.7) | data formatting | bytes 1048576
  75.8 0.8 %copy.13 = bf16[1,128,2048]{2,1,0:T(8,128)(2,1)} copy(bf16[1,128,2048]{2,1,0:T(8,128)(2,1)S(1)} %bitcast.6) | data formatting | bytes 1048576
  76.6 0.8 copy.14

commit v3 on v2

--- a/solution.py
+++ b/solution.py
@@ -40,14 +40,14 @@
     return lax.dot_general(a, b, (((1,), (0,)), ((), ())), preferred_element_type=F32)
 
 
-NSEM = 192
+NSEM = 208
 
 
 def kernel(
     q_hbm, g_hbm, enc_hbm, w_hbm, ids_s, slot_s,
     attv, dqv, gout,
     wbuf, encbuf, qg, qgw, xrd, pbuf, dsbuf, acc, own16, sib16,
-    xsend, xrecv, zsend, zrecv, px, ids_v, sibids_v, sibids_s,
+    xsend, xrecv, zsend, zrecv, bzs, bzr, bfs, bfr, bns, bnr, px, ids_v, sibids_v, sibids_s,
     ssem, rsem, lsem,
 ):
     dp = lax.axis_index("dp")
@@ -412,16 +412,16 @@
         total = own16[0, which(pos, 0, p), rows].astype(F32) + own16[1, which(pos, 1, p), rows].astype(F32)
         return total + (sib16[0, which(spos, 0, p), rows].astype(F32) + sib16[1, which(spos, 1, p), rows].astype(F32))
 
-    TOP, BOT = slice(0, 32), slice(32, 64)
+    NA = NLEN // 2
+    TOP, BOT, ROWB = slice(0, NA // 2), slice(NA // 2, NA), slice(NA, NLEN)
     DIRS = (("r", right_x, left_x, 1, TOP, BOT), ("l", left_x, right_x, -1, BOT, TOP))
 
     def far(half):
         for di, (nm, to, _, sg, mine, _) in enumerate(DIRS):
-            m = 0 if half == 0 else 1
             zz = 1 - zl if half == 0 else zl
             for j in range(2):
-                xsend[di, m, j] = chip_sum(2, zz, j, mine).astype(BF)
-            send(2, ("x", m, nm), xsend.at[di, m], xrecv.at[di, m], to)
+                xsend[di, half, j] = chip_sum(2, zz, j, mine).astype(BF)
+            send(2, ("x", half, nm), xsend.at[di, half], xrecv.at[di, half], to)
 
     def near(half):
         for di, (nm, to, _, sg, _, other) in enumerate(DIRS):
@@ -456,22 +456,66 @@
                 gout[j, TOP] = top
                 gout[j, BOT] = bot
 
+    COLS = (2, 1, -1, 0)
+
+    def b_z(i):
+        for j in range(2):
+            bzs[i, j] = chip_sum(COLS[i], 1 - zl, j, ROWB).astype(BF)
+        send(2, ("bz", i), bzs.at[i], bzr.at[i], inner)
+
+    def b_sum(i, j):
+        return chip_sum(COLS[i], zl, j, ROWB) + bzr[i, j].astype(F32)
+
+    def b_far():
+        recv(("bz", 0), bzr.at[0], inner)
+        for di, (nm, to, _, _, _, _) in enumerate(DIRS):
+            bfs[di] = b_sum(0, di).astype(BF)
+            send(2, ("bf", nm), bfs.at[di], bfr.at[di], to)
+
+    def b_near():
+        for di, (nm, to, _, _, _, _) in enumerate(DIRS):
+            recv(("bz", 1 + di), bzr.at[1 + di], inner)
+            bns[di, 1 - di] = b_sum(1 + di, 1 - di).astype(BF)
+            send(2, ("bn", nm, 0), bns.at[di, 1 - di], bnr.at[di, 1 - di], to)
+
+    def b_near_add():
+        for di, (nm, to, frm, _, _, _) in enumerate(DIRS):
+            recv(("bf", nm), bfr.at[di], frm)
+            bns[di, di] = (b_sum(1 + di, di) + bfr[di].astype(F32)).astype(BF)
+            send(2, ("bn", nm, 1), bns.at[di, di], bnr.at[di, di], to)
+
+    def b_total():
+        recv(("bz", 3), bzr.at[3], inner)
+        for di, (nm, _, frm, _, _, _) in enumerate(DIRS):
+            recv(("bn", nm, 0), bnr.at[di, 1 - di], frm)
+            recv(("bn", nm, 1), bnr.at[di, di], frm)
+        for j in range(2):
+            gout[j, ROWB] = b_sum(3, j) + bnr[0, j].astype(F32) + bnr[1, j].astype(F32)
+
     outputs(1)
     recv(("rs",), sib16.at[:, 0:2], sib)
     far(0)
+    b_z(0)
+    far(1)
+    b_z(1)
+    b_z(2)
     near(0)
-    far(1)
+    b_z(3)
     outputs(-1)
     near_add(0)
     near(1)
+    b_far()
     near_add(1)
-    outputs(0)
+    b_near()
+    b_near_add()
     total(0)
     send(2, ("rz",), zsend, zrecv, inner)
+    outputs(0)
     total(1)
+    b_total()
     recv(("rz",), zrecv, inner)
     for j in range(2):
-        gout[j] = gout[j] + zrecv[j].astype(F32)
+        gout[j, 0:NA] = gout[j, 0:NA] + zrecv[j].astype(F32)
 
     def drain(items):
         for i, src, dev in items:
@@ -512,10 +556,16 @@
             pltpu.VMEM((2, 2 * NLEN, DE), F32),
             pltpu.VMEM((2, 3, NLEN, DE), BF),
             pltpu.VMEM((2, 3, NLEN, DE), BF),
-            pltpu.VMEM((2, 6, 2, 32, DE), BF),
-            pltpu.VMEM((2, 6, 2, 32, DE), BF),
-            pltpu.VMEM((2, NLEN, DE), BF),
-            pltpu.VMEM((2, NLEN, DE), BF),
+            pltpu.VMEM((2, 6, 2, NLEN // 4, DE), BF),
+            pltpu.VMEM((2, 6, 2, NLEN // 4, DE), BF),
+            pltpu.VMEM((2, NLEN // 2, DE), BF),
+            pltpu.VMEM((2, NLEN // 2, DE), BF),
+            pltpu.VMEM((4, 2, NLEN // 2, DE), BF),
+            pltpu.VMEM((4, 2, NLEN // 2, DE), BF),
+            pltpu.VMEM((2, NLEN // 2, DE), BF),
+            pltpu.VMEM((2, NLEN // 2, DE), BF),
+            pltpu.VMEM((2, 2, NLEN // 2, DE), BF),
+            pltpu.VMEM((2, 2, NLEN // 2, DE), BF),
             pltpu.VMEM((2, 4, 2, SPAN, DE), BF),
             pltpu.VMEM((8, 128), jnp.int32),
             pltpu.VMEM((8, 128), jnp.int32),

time: 77.5 us -> 73.8 us (0.952)
  Pallas kernels: 74.3 us -> 70.6 us
    pallas_call x1, Pallas kernels: 74.3 us -> 70.6 us  [per_device(): pl.pallas_call(kernel, out_shape=(pltpu.VMEM((2 * SPAN, HEADS * HS), BF),...]
where the time goes in v3:
time: 73.8 us; the launch traced here: 73.6 us
  Pallas kernels  70.6 us (96%)
  local copies, waits for them, and re-layouts  2.36 us (3%)
    pallas_call x1, Pallas kernels, per_device(): pl.pallas_call(kernel, out_shape=(pltpu.VMEM((2 * SPAN, HEADS * HS), BF),...  70.6 us
    unnamed x3, local copies, waits for them, and re-layouts  2.36 us

profile of v3, /device:TPU:24, one launch (start us, length us, event | category | flops | bytes accessed | tf_op | source)
XLA Modules:
  0.0 73.6 jit_solution(399675493235571316)
XLA Ops:
  0.6 70.6 %shard_map.85 = (bf16[128,2048]{1,0:T(8,128)(2,1)S(1)}, bf16[128,2048]{1,0:T(8,128)(2,1)S(1)}, f32[2,64,896]{2,1,0:T(8,128)S(1)}) custom-call(bf16[128,2048]{1,0:T(8,128)(2,1)} %bitcast.9, bf16[128,2048]{1,0:T(8,128)(2,1)} %bitcast.10, bf16[2,64,896]{2,1,0:T(8,128)(2,1)} %bitcast.11, bf16[896,128]{1,0:T(8,128)(2,1)} %w_hbm.1, s32[1,2,2]{2,1,0:T(2,128)} %ids_s.1, ...), custom_call_target="tpu_custom_call" | custom-call | tf_op jit(solution)/shard_map/pallas_call | solution.py:539
  71.3 0.8 %copy.12 = bf16[1,128,2048]{2,1,0:T(8,128)(2,1)} copy(bf16[1,128,2048]{2,1,0:T(8,128)(2,1)S(1)} %bitcast.7) | data formatting | bytes 1048576
  72.1 0.8 %copy.13 = bf16[1,128,2048]{2,1,0:T(8,128)(2,1)} copy(bf16[1,128,2048]{2,1,0:T(8,128)(2,1)S(1)} %bitcast.6) | data formatting | bytes 1048576
  72.9 0.8 %copy.14 = f32[1,2,64,896]{3,2,1,0:T(8,128)} copy(f32[1,2,64,896]{3,2,1,0:T(8,128)S(1)} %bitcast.8) | data formatting | bytes 917504

commit v4 on v3

--- a/solution.py
+++ b/solution.py
@@ -386,7 +386,6 @@
     from_sib((-3,))
     project(-3)
     attend(1, False)
-    outputs(2)
     cp.wait()
     stage(11)
     from_sib((3,))
@@ -502,6 +501,7 @@
     near(0)
     b_z(3)
     outputs(-1)
+    outputs(2)
     near_add(0)
     near(1)
     b_far()

time: 73.8 us -> 72.7 us (0.985)
  Pallas kernels: 70.6 us -> 69.6 us
    pallas_call x1, Pallas kernels: 70.6 us -> 69.6 us  [per_device(): pl.pallas_call(kernel, out_shape=(pltpu.VMEM((2 * SPAN, HEADS * HS), BF),...]
where the time goes in v4:
time: 72.7 us; the launch traced here: 72.6 us
  Pallas kernels  69.6 us (96%)
  local copies, waits for them, and re-layouts  2.36 us (3%)
    pallas_call x1, Pallas kernels, per_device(): pl.pallas_call(kernel, out_shape=(pltpu.VMEM((2 * SPAN, HEADS * HS), BF),...  69.6 us
    unnamed x3, local copies, waits for them, and re-layouts  2.36 us

profile of v4, /device:TPU:24, one launch (start us, length us, event | category | flops | bytes accessed | tf_op | source)
XLA Modules:
  0.0 72.6 jit_solution(8944411531707732445)
XLA Ops:
  0.6 69.6 %shard_map.85 = (bf16[128,2048]{1,0:T(8,128)(2,1)S(1)}, bf16[128,2048]{1,0:T(8,128)(2,1)S(1)}, f32[2,64,896]{2,1,0:T(8,128)S(1)}) custom-call(bf16[128,2048]{1,0:T(8,128)(2,1)} %bitcast.9, bf16[128,2048]{1,0:T(8,128)(2,1)} %bitcast.10, bf16[2,64,896]{2,1,0:T(8,128)(2,1)} %bitcast.11, bf16[896,128]{1,0:T(8,128)(2,1)} %w_hbm.1, s32[1,2,2]{2,1,0:T(2,128)} %ids_s.1, ...), custom_call_target="tpu_custom_call" | custom-call | tf_op jit(solution)/shard_map/pallas_call | solution.py:539
  70.2 0.8 %copy.12 = bf16[1,128,2048]{2,1,0:T(8,128)(2,1)} copy(bf16[1,128,2048]{2,1,0:T(8,128)(2,1)S(1)} %bitcast.7) | data formatting | bytes 1048576
  71.0 0.8 %copy.13 = bf16[1,128,2048]{2,1,0:T(8,128)(2,1)} copy(bf16[1,128,2048]{2,1,0:T(8,128)(2,1)S(1)} %bitcast.6) | data formatting | bytes 1048576
  71.8 0.8 %copy.14 = f32[1,2,64,896]{3,2,1,0:T(8,128)} copy(f32[1,2,64,896]{3,2,1,0:T(8,128)S(1)} %bitcast.8) | data formatting | bytes 917504
